TPU v7x, 32 devices: a whole 2x2x4 slice. The times are simulated.
32 devices in a mesh: dp: 8 (over z, y), tp: 4 (over x, core).
Axes of the slice: x: 2, y: 2, z: 4, core: 2. Of those that a mesh axis runs over, the one named last changes fastest.
Arguments:
- frames: bfloat16 [16, 2304, 384], P('dp', 'tp'), may hold values from -6 to 6
- targets: bfloat16 [16, 2304, 384], P('dp', 'tp'), may hold values from -6 to 6
- presence: int32 [16, 4], P('dp'), may hold values 0 or 1
- order: int32 [8, 2], P('dp'), may hold values from 0 to 1, each once within a row
- attn_proj: float32 [3, 384, 384], P(None, None, 'tp'), may hold values from -0.3125 to 0.3125
- out_proj: float32 [384, 384], P('tp'), may hold values from -7 to 7
- up_proj: float32 [384, 1536], P(None, 'tp'), may hold values from -0.3125 to 0.3125
- up_bias: float32 [1536], P('tp'), may hold values from -3 to 3
- down_proj: float32 [384, 1536], P(None, 'tp'), may hold values from -0.15625 to 0.15625
- head_proj: float32 [384, 384], replicated, may hold values from -0.3125 to 0.3125
- vectors: float32 [9, 384], replicated
- momentum_attn: float32 [3, 384, 384], P(None, None, 'tp'), may hold values from -256 to 256
- momentum_out: float32 [384, 384], P('tp'), may hold values from -3 to 3
- momentum_up: float32 [384, 1536], P(None, 'tp'), may hold values from -3 to 3
- momentum_bias: float32 [1536], P('tp'), may hold values from -3 to 3
- momentum_down: float32 [384, 1536], P(None, 'tp'), may hold values from -3 to 3
- momentum_head: float32 [384, 384], replicated, may hold values from -224 to 224
- momentum_vectors: float32 [9, 384], replicated, may hold values from -3 to 3
- average_attn: float32 [3, 384, 384], P(None, None, 'tp'), may hold values from -0.3125 to 0.3125
- average_out: float32 [384, 384], P('tp'), may hold values from -7 to 7
- average_up: float32 [384, 1536], P(None, 'tp'), may hold values from -0.3125 to 0.3125
- average_bias: float32 [1536], P('tp'), may hold values from -3 to 3
- average_down: float32 [384, 1536], P(None, 'tp'), may hold values from -0.15625 to 0.15625
- average_head: float32 [384, 384], replicated, may hold values from -0.3125 to 0.3125
- average_vectors: float32 [9, 384], replicated
Outputs:
- loss: float32 [], replicated
- new_attn: float32 [3, 384, 384], P(None, None, 'tp')
- new_out: float32 [384, 384], P('tp')
- new_up: float32 [384, 1536], P(None, 'tp')
- new_bias: float32 [1536], P('tp')
- new_down: float32 [384, 1536], P(None, 'tp')
- new_head: float32 [384, 384], replicated
- new_vectors: float32 [9, 384], replicated
- moment_attn: float32 [3, 384, 384], P(None, None, 'tp')
- moment_out: float32 [384, 384], P('tp')
- moment_up: float32 [384, 1536], P(None, 'tp')
- moment_bias: float32 [1536], P('tp')
- moment_down: float32 [384, 1536], P(None, 'tp')
- moment_head: float32 [384, 384], replicated
- moment_vectors: float32 [9, 384], replicated
- mean_attn: float32 [3, 384, 384], P(None, None, 'tp')
- mean_out: float32 [384, 384], P('tp')
- mean_up: float32 [384, 1536], P(None, 'tp')
- mean_bias: float32 [1536], P('tp')
- mean_down: float32 [384, 1536], P(None, 'tp')
- mean_head: float32 [384, 384], replicated
- mean_vectors: float32 [9, 384], replicated
- grad_frames: float32 [16, 2304, 384], P('dp', 'tp')
Inputs may be any that keep to these rules, and one draw needn't show every extreme that they name: `order`: each row holds every number below 2 once.
All inputs are finite; a program needn't handle non-finite values. No bound on the sum of `presence` on one device may be relied on, other than what follows from the above.
Results may differ from a plain program's by a relative error of at most 0.0095.
Values may be sent and summed in bfloat16 or wider, within the bound.
No kernel may reach another device: no remote copies, remote signals or barrier semaphores. Data moves between devices by JAX's collectives and lax.ppermute only.
A program may use at most 192 MiB of HBM per device.

v0:
```python
import jax
import jax.numpy as jnp
from jax import lax
from jax.sharding import PartitionSpec as P

CHN = 96
HDIM = 48
HEAD = 384
EPSILON = 1e-05
MOMENTUM_RATE = 0.9
LEARN_RATE = 0.02
AVERAGE_RATE = 0.9


def product(left, right, form):
    return jnp.einsum(form, left, right, preferred_element_type=jnp.float32)


def norm_forward(values, gain, shift):
    centred = values - jnp.mean(values, axis=-1, keepdims=True)
    inverse = lax.rsqrt(jnp.mean(centred * centred, axis=-1, keepdims=True) + EPSILON)
    normed = centred * inverse
    return (normed * gain + shift, normed, inverse)


def norm_backward(grad, normed, inverse, gain):
    scaled = grad * gain
    back = inverse * (
        scaled
        - jnp.mean(scaled, axis=-1, keepdims=True)
        - normed * jnp.mean(scaled * normed, axis=-1, keepdims=True)
    )
    return (back, jnp.sum(grad * normed, axis=(0, 1)), jnp.sum(grad, axis=(0, 1)))


def head_forward(packed):
    query_rows, key_rows, value_rows = packed
    scores = product(query_rows, key_rows, "qd,kd->qk") * HDIM ** (-0.5)
    maximum = jnp.max(scores, axis=-1, keepdims=True)
    exponent = jnp.exp(scores - maximum)
    totals = jnp.sum(exponent, axis=-1, keepdims=True)
    weights = (exponent / totals).astype(jnp.bfloat16)
    mixed = product(weights, value_rows, "qk,kd->qd").astype(jnp.bfloat16)
    return (mixed, (maximum + jnp.log(totals))[:, 0])


def head_backward(packed):
    query_rows, key_rows, value_rows, logsum, grad_out = packed
    factor = HDIM ** (-0.5)
    probs = jnp.exp(product(query_rows, key_rows, "qd,kd->qk") * factor - logsum[:, None])
    grad_value = product(probs.astype(jnp.bfloat16), grad_out, "qk,qd->kd")
    grad_probs = product(grad_out, value_rows, "qd,kd->qk")
    grad_scores = (
        probs * (grad_probs - jnp.sum(probs * grad_probs, axis=-1, keepdims=True))
    ).astype(jnp.bfloat16)
    grad_query = product(grad_scores, key_rows, "qk,kd->qd") * factor
    grad_key = product(grad_scores, query_rows, "qk,qd->kd") * factor
    return jnp.stack([grad_query, grad_key, grad_value]).astype(jnp.bfloat16)


def to_heads(packed, items, heads_here):
    length = packed.shape[2]
    split = packed.reshape(3, items, length, heads_here, HDIM).transpose(0, 1, 3, 2, 4)
    return split.reshape(3, items * heads_here, length, HDIM)


def from_heads(stacked, items, heads_here):
    length = stacked.shape[-2]
    split = stacked.reshape(stacked.shape[:-3] + (items, heads_here, length, HDIM))
    moved = jnp.moveaxis(split, -2, -3)
    return moved.reshape(stacked.shape[:-3] + (items, length, heads_here * HDIM))


def update(weight, moment, average, grad):
    moment_new = MOMENTUM_RATE * moment + grad
    weight_new = weight - LEARN_RATE * (grad + MOMENTUM_RATE * moment_new)
    average_new = AVERAGE_RATE * average + (1.0 - AVERAGE_RATE) * weight_new
    return (weight_new, moment_new, average_new)


def per_device(
    frames,
    targets,
    presence,
    order,
    attn_proj,
    out_proj,
    up_proj,
    up_bias,
    down_proj,
    head_proj,
    vectors,
    momentum_attn,
    momentum_out,
    momentum_up,
    momentum_bias,
    momentum_down,
    momentum_head,
    momentum_vectors,
    average_attn,
    average_out,
    average_up,
    average_bias,
    average_down,
    average_head,
    average_vectors,
):
    items = frames.shape[0]
    heads_here = out_proj.shape[0] // HDIM
    bf16 = jnp.bfloat16
    start = frames.astype(jnp.float32)
    goal = jnp.take(targets, order[0], axis=0).astype(jnp.float32)
    keep = (presence.astype(jnp.float32)[:, :, None] * jnp.ones((1, 1, CHN), jnp.float32)).reshape(
        items, 1, HEAD
    )
    head_low = head_proj.astype(bf16)
    attn_low = attn_proj.astype(bf16)
    out_low = out_proj.astype(bf16)
    first, hat_one, inv_one = norm_forward(start, vectors[0], vectors[1])
    first_low = first.astype(bf16)
    first_all = lax.all_gather(first_low, "tp", axis=1, tiled=True)
    packed = product(first_all, attn_low, "bsd,jde->jbse").astype(bf16)
    heads = to_heads(packed, items, heads_here)
    mixed, logsum = lax.map(head_forward, (heads[0], heads[1], heads[2]))
    attended = from_heads(mixed, items, heads_here)
    attn_term = lax.psum_scatter(
        product(attended, out_low, "bse,ed->bsd"), "tp", scatter_dimension=1, tiled=True
    )
    middle = start + vectors[3] * (attn_term + vectors[2])
    second, hat_two, inv_two = norm_forward(middle, vectors[4], vectors[5])
    second_low = second.astype(bf16)
    up_all = up_proj.astype(bf16)
    down_all = down_proj.astype(bf16)
    second_all = lax.all_gather(second_low, "tp", axis=1, tiled=True)
    hidden_pre = product(second_all, up_all, "bsd,df->bsf") + up_bias
    hidden = jax.nn.gelu(hidden_pre).astype(bf16)
    ffn_term = lax.psum_scatter(
        product(hidden, down_all, "bsf,df->bsd"), "tp", scatter_dimension=1, tiled=True
    )
    final = middle + vectors[7] * (ffn_term + vectors[6])
    final_low = final.astype(bf16)
    pred = product(final_low, head_low, "bsd,dh->bsh") + vectors[8]
    diff = pred - goal
    smooth = jnp.sqrt(diff * diff + 1.0)
    part_loss = jnp.sum(keep * (smooth - 1.0)) / HEAD
    grad_pred = (keep * (diff / smooth) / HEAD).astype(bf16)
    grad_head = product(final_low, grad_pred, "bsd,bsh->dh")
    grad_head_bias = jnp.sum(grad_pred.astype(jnp.float32), axis=(0, 1))
    grad_final = product(grad_pred, head_low, "bsh,dh->bsd")
    grad_scale_two = jnp.sum(grad_final * (ffn_term + vectors[6]), axis=(0, 1))
    grad_ffn = grad_final * vectors[7]
    grad_down_bias = jnp.sum(grad_ffn, axis=(0, 1))
    ffn_low = grad_ffn.astype(bf16)
    gelu_pull = jax.vjp(jax.nn.gelu, hidden_pre)[1]
    ffn_all = lax.all_gather(ffn_low, "tp", axis=1, tiled=True)
    grad_hidden = product(ffn_all, down_all, "bsd,df->bsf")
    grad_down = product(ffn_all, hidden, "bsd,bsf->df")
    grad_pre = gelu_pull(grad_hidden)[0].astype(bf16)
    grad_up = product(second_all, grad_pre, "bsd,bsf->df")
    grad_up_bias = jnp.sum(grad_pre.astype(jnp.float32), axis=(0, 1))
    grad_second = lax.psum_scatter(
        product(grad_pre, up_all, "bsf,df->bsd"), "tp", scatter_dimension=1, tiled=True
    )
    back_two, grad_gain_two, grad_shift_two = norm_backward(
        grad_second, hat_two, inv_two, vectors[4]
    )
    grad_middle = grad_final + back_two
    grad_scale_one = jnp.sum(grad_middle * (attn_term + vectors[2]), axis=(0, 1))
    grad_attn = grad_middle * vectors[3]
    grad_out_bias = jnp.sum(grad_attn, axis=(0, 1))
    attn_grad_low = grad_attn.astype(bf16)
    attn_all = lax.all_gather(attn_grad_low, "tp", axis=1, tiled=True)
    grad_out = product(attended, attn_all, "bse,bsd->ed")
    grad_attended = product(attn_all, out_low, "bsd,ed->bse").astype(bf16)
    grad_mixed = to_heads(jnp.stack([grad_attended] * 3), items, heads_here)[0]
    grad_heads = lax.map(head_backward, (heads[0], heads[1], heads[2], logsum, grad_mixed))
    grad_packed = from_heads(jnp.moveaxis(grad_heads, 1, 0), items, heads_here)
    grad_attn_proj = product(first_all, grad_packed, "bsd,jbse->jde")
    grad_first = lax.psum_scatter(
        product(grad_packed, attn_low, "jbse,jde->bsd").astype(jnp.bfloat16),
        "tp",
        scatter_dimension=1,
        tiled=True,
    ).astype(jnp.float32)
    back_one, grad_gain_one, grad_shift_one = norm_backward(
        grad_first, hat_one, inv_one, vectors[0]
    )
    grad_frames = grad_middle + back_one
    grad_vectors = jnp.stack(
        [
            grad_gain_one,
            grad_shift_one,
            grad_out_bias,
            grad_scale_one,
            grad_gain_two,
            grad_shift_two,
            grad_down_bias,
            grad_scale_two,
            grad_head_bias,
        ]
    )
    grad_attn_proj, grad_out, grad_up, grad_up_bias, grad_down = lax.psum(
        (grad_attn_proj, grad_out, grad_up, grad_up_bias, grad_down), "dp"
    )
    grad_head, grad_vectors, loss = lax.psum((grad_head, grad_vectors, part_loss), ("dp", "tp"))
    first_set = update(attn_proj, momentum_attn, average_attn, grad_attn_proj)
    second_set = update(out_proj, momentum_out, average_out, grad_out)
    third_set = update(up_proj, momentum_up, average_up, grad_up)
    fourth_set = update(up_bias, momentum_bias, average_bias, grad_up_bias)
    fifth_set = update(down_proj, momentum_down, average_down, grad_down)
    sixth_set = update(head_proj, momentum_head, average_head, grad_head)
    seventh_set = update(vectors, momentum_vectors, average_vectors, grad_vectors)
    return (
        loss,
        first_set[0],
        second_set[0],
        third_set[0],
        fourth_set[0],
        fifth_set[0],
        sixth_set[0],
        seventh_set[0],
        first_set[1],
        second_set[1],
        third_set[1],
        fourth_set[1],
        fifth_set[1],
        sixth_set[1],
        seventh_set[1],
        first_set[2],
        second_set[2],
        third_set[2],
        fourth_set[2],
        fifth_set[2],
        sixth_set[2],
        seventh_set[2],
        grad_frames,
    )


def solution(mesh):
    in_specs = (
        P("dp", "tp", None),
        P("dp", "tp", None),
        P("dp", None),
        P("dp", None),
        P(None, None, "tp"),
        P("tp", None),
        P(None, "tp"),
        P("tp"),
        P(None, "tp"),
        P(),
        P(),
        P(None, None, "tp"),
        P("tp", None),
        P(None, "tp"),
        P("tp"),
        P(None, "tp"),
        P(),
        P(),
        P(None, None, "tp"),
        P("tp", None),
        P(None, "tp"),
        P("tp"),
        P(None, "tp"),
        P(),
        P(),
    )
    out_specs = (
        P(),
        P(None, None, "tp"),
        P("tp", None),
        P(None, "tp"),
        P("tp"),
        P(None, "tp"),
        P(),
        P(),
        P(None, None, "tp"),
        P("tp", None),
        P(None, "tp"),
        P("tp"),
        P(None, "tp"),
        P(),
        P(),
        P(None, None, "tp"),
        P("tp", None),
        P(None, "tp"),
        P("tp"),
        P(None, "tp"),
        P(),
        P(),
        P("dp", "tp", None),
    )
    return jax.shard_map(
        per_device, mesh=mesh, in_specs=in_specs, out_specs=out_specs, check_vma=False
    )
```

profile of v0, /device:TPU:0, one launch (start us, length us, event | category | flops | bytes accessed | tf_op | source)
XLA Modules:
  0.0 926.0 jit_solution(6012306189877405584)
XLA Ops:
  14.3 33.5 %all-gather.5.cloned.1.call-done = bf16[2,2304,384]{2,1,0:T(8,128)(2,1)} async-done(((bf16[2,576,384]{2,1,0:T(8,128)(2,1)}), bf16[2,2304,384]{2,1,0:T(8,128)(2,1)}) %all-gather.5.cloned.1.call-update) | async-done | bytes 3538960 | tf_op jit(solution)/shard_map/all_gather | solution.py:121
  61.8 57.2 %while.22 = (s32[]{:T(128)}, bf16[4,2304,48]{1,2,0:T(8,128)(2,1)}, f32[4,2304]{1,0:T(4,128)}, bf16[4,2304,48]{2,1,0:T(8,128)(2,1)S(1)}, bf16[4,2304,48]{2,1,0:T(...) while((s32[]{:T(128)}, bf16[4,2304,48]{1,2,0:T(8,128)(2,1)}, f32[4,2304]{1,0:T(4,128)}, ...), condition=%wide.region_5.6_spmd, body=%wide.region_2.0_spmd.sunk | while | flops 1056483072 | bytes 65804384 | solution.py:124
  124.9 63.7 %reduce-scatter.5.cloned.1.call-done = f32[2,576,384]{2,1,0:T(8,128)} async-done(((f32[2,2304,384]{2,1,0:T(8,128)}), f32[2,576,384]{2,1,0:T(8,128)}) %reduce-scatter.5.cloned.1.call-update) | async-done | bytes 1769488 | tf_op jit(solution)/shard_map/reduce_scatter | solution.py:126
  192.6 30.7 %all-gather.7.cloned.1.call-done = bf16[2,2304,384]{2,1,0:T(8,128)(2,1)} async-done(((bf16[2,576,384]{2,1,0:T(8,128)(2,1)}), bf16[2,2304,384]{2,1,0:T(8,128)(2,1)}) %all-gather.7.cloned.1.call-update) | async-done | bytes 3538960 | tf_op jit(solution)/shard_map/all_gather | solution.py:134
  237.9 61.4 %reduce-scatter.7.cloned.1.call-done = f32[2,576,384]{2,1,0:T(8,128)} async-done(((f32[2,2304,384]{2,1,0:T(8,128)}), f32[2,576,384]{2,1,0:T(8,128)}) %reduce-scatter.7.cloned.1.call-update) | async-done | bytes 1769488 | tf_op jit(solution)/shard_map/reduce_scatter | solution.py:137
  307.0 30.7 %all-gather.9.cloned.1.call-done = bf16[2,2304,384]{2,1,0:T(8,128)(2,1)} async-done(((bf16[2,576,384]{2,1,0:T(8,128)(2,1)}), bf16[2,2304,384]{2,1,0:T(8,128)(2,1)}) %all-gather.9.cloned.1.call-update) | async-done | bytes 3538960 | tf_op jit(solution)/shard_map/all_gather | solution.py:155
  353.9 63.8 %reduce-scatter.9.cloned.1.call-done = f32[2,576,384]{2,1,0:T(8,128)} async-done(((f32[2,2304,384]{2,1,0:T(8,128)}), f32[2,576,384]{2,1,0:T(8,128)}) %reduce-scatter.9.cloned.1.call-update) | async-done | bytes 1769488 | tf_op jit(solution)/shard_map/reduce_scatter | solution.py:161
  438.8 18.2 %all-gather.11.cloned.1.call-done = bf16[2,2304,384]{2,1,0:T(8,128)(2,1)} async-done(((bf16[2,576,384]{2,1,0:T(8,128)(2,1)}), bf16[2,2304,384]{2,1,0:T(8,128)(2,1)}) %all-gather.11.cloned.1.call-update) | async-done | bytes 3538960 | tf_op jit(solution)/shard_map/all_gather | solution.py:172
  463.4 263.5 %while.23 = (s32[]{:T(128)}, bf16[4,3,2304,48]{2,3,1,0:T(8,128)(2,1)}, bf16[4,2304,48]{2,1,0:T(8,128)(2,1)S(1)}, bf16[4,2304,48]{2,1,0:T(8,128)(2,1)}, f32[4,230...) while((s32[]{:T(128)}, ...), condition=%wide.region_17.18_spmd, body=%wide.region_15.17_spmd.sunk | while | flops 2593048320 | bytes 211429520 | solution.py:176
  464.2 11.4 %fusion.152 = f32[2304,2304]{0,1:T(8,128)} fusion(bf16[4,2304,48]{2,1,0:T(8,128)(2,1)} %get-tuple-element.366, s32[]{:T(128)S(6)} %copy.111, bf16[4,2304,48]{2,1,0:T(8,128)(2,1)} %get-tuple-element.365), kind=kOutput, calls=%fused_computation.33.clone.1 | convolution fusion | flops 509607936 | bytes 22414336 | tf_op jit(solution)/shard_map/while/body/eval_jaxpr/qd,kd->qk/dot_general | solution.py:16
  475.7 13.6 %multiply_reduce_fusion.11 = (f32[2304]{0:T(1024)S(1)}, f32[2304,2304]{0,1:T(8,128)}) fusion(f32[2304,2304]{0,1:T(8,128)} %fusion.152, f32[2304]{0:T(1024)S(1)} %dynamic-slice_reduce_fusion.2, bf16[4,2304,48]{2,1,0:T(8,128)(2,1)S(1)} %copy-done.5, s32[]{:T(128)S(6)} %copy.111, bf16[4,2304,48]{2,1,0:T(8,128)(2,1)S(1)} %get-tuple-element.362), kind=kOutput, calls=%fused_computation.20.clone.1 | convolution fusion | flops 530839296 | bytes 43669504 | tf_op jit(solution)/shard_map/while/body/eval_jaxpr/qd,kd->qk/dot_general | solution.py:16
  489.3 18.4 %multiply_convert_fusion.9 = bf16[2304,2304]{0,1:T(8,128)(2,1)} fusion(f32[2304,2304]{0,1:T(8,128)} %get-tuple-element.318, f32[2304,2304]{0,1:T(8,128)} %fusion.152, f32[2304]{0:T(1024)S(1)} %get-tuple-element.319), kind=kLoop, calls=%fused_computation.19.clone.1 | loop fusion | flops 15925248 | bytes 53093376 | tf_op jit(solution)/shard_map/while/body/eval_jaxpr/convert_element_type | solution.py:55
  530.3 11.4 %fusion.152 = f32[2304,2304]{0,1:T(8,128)} fusion(bf16[4,2304,48]{2,1,0:T(8,128)(2,1)} %get-tuple-element.366, s32[]{:T(128)S(6)} %copy.111, bf16[4,2304,48]{2,1,0:T(8,128)(2,1)} %get-tuple-element.365), kind=kOutput, calls=%fused_computation.33.clone.1 | convolution fusion | flops 509607936 | bytes 22414336 | tf_op jit(solution)/shard_map/while/body/eval_jaxpr/qd,kd->qk/dot_general | solution.py:16
  541.8 13.6 %multiply_reduce_fusion.11 = (f32[2304]{0:T(1024)S(1)}, f32[2304,2304]{0,1:T(8,128)}) fusion(f32[2304,2304]{0,1:T(8,128)} %fusion.152, f32[2304]{0:T(1024)S(1)} %dynamic-slice_reduce_fusion.2, bf16[4,2304,48]{2,1,0:T(8,128)(2,1)S(1)} %copy-done.5, s32[]{:T(128)S(6)} %copy.111, bf16[4,2304,48]{2,1,0:T(8,128)(2,1)S(1)} %get-tuple-element.362), kind=kOutput, calls=%fused_computation.20.clone.1 | convolution fusion | flops 530839296 | bytes 43669504 | tf_op jit(solution)/shard_map/while/body/eval_jaxpr/qd,kd->qk/dot_general | solution.py:16
  555.3 18.4 %multiply_convert_fusion.9 = bf16[2304,2304]{0,1:T(8,128)(2,1)} fusion(f32[2304,2304]{0,1:T(8,128)} %get-tuple-element.318, f32[2304,2304]{0,1:T(8,128)} %fusion.152, f32[2304]{0:T(1024)S(1)} %get-tuple-element.319), kind=kLoop, calls=%fused_computation.19.clone.1 | loop fusion | flops 15925248 | bytes 53093376 | tf_op jit(solution)/shard_map/while/body/eval_jaxpr/convert_element_type | solution.py:55
  607.6 13.5 %multiply_reduce_fusion.11 = (f32[2304]{0:T(1024)S(1)}, f32[2304,2304]{0,1:T(8,128)}) fusion(f32[2304,2304]{0,1:T(8,128)} %fusion.152, f32[2304]{0:T(1024)S(1)} %dynamic-slice_reduce_fusion.2, bf16[4,2304,48]{2,1,0:T(8,128)(2,1)S(1)} %copy-done.5, s32[]{:T(128)S(6)} %copy.111, bf16[4,2304,48]{2,1,0:T(8,128)(2,1)S(1)} %get-tuple-element.362), kind=kOutput, calls=%fused_computation.20.clone.1 | convolution fusion | flops 530839296 | bytes 43669504 | tf_op jit(solution)/shard_map/while/body/eval_jaxpr/qd,kd->qk/dot_general | solution.py:16
  621.2 18.3 %multiply_convert_fusion.9 = bf16[2304,2304]{0,1:T(8,128)(2,1)} fusion(f32[2304,2304]{0,1:T(8,128)} %get-tuple-element.318, f32[2304,2304]{0,1:T(8,128)} %fusion.152, f32[2304]{0:T(1024)S(1)} %get-tuple-element.319), kind=kLoop, calls=%fused_computation.19.clone.1 | loop fusion | flops 15925248 | bytes 53093376 | tf_op jit(solution)/shard_map/while/body/eval_jaxpr/convert_element_type | solution.py:55
  661.9 11.4 %fusion.152 = f32[2304,2304]{0,1:T(8,128)} fusion(bf16[4,2304,48]{2,1,0:T(8,128)(2,1)} %get-tuple-element.366, s32[]{:T(128)S(6)} %copy.111, bf16[4,2304,48]{2,1,0:T(8,128)(2,1)} %get-tuple-element.365), kind=kOutput, calls=%fused_computation.33.clone.1 | convolution fusion | flops 509607936 | bytes 22414336 | tf_op jit(solution)/shard_map/while/body/eval_jaxpr/qd,kd->qk/dot_general | solution.py:16
  673.3 13.5 %multiply_reduce_fusion.11 = (f32[2304]{0:T(1024)S(1)}, f32[2304,2304]{0,1:T(8,128)}) fusion(f32[2304,2304]{0,1:T(8,128)} %fusion.152, f32[2304]{0:T(1024)S(1)} %dynamic-slice_reduce_fusion.2, bf16[4,2304,48]{2,1,0:T(8,128)(2,1)S(1)} %copy-done.5, s32[]{:T(128)S(6)} %copy.111, bf16[4,2304,48]{2,1,0:T(8,128)(2,1)S(1)} %get-tuple-element.362), kind=kOutput, calls=%fused_computation.20.clone.1 | convolution fusion | flops 530839296 | bytes 43669504 | tf_op jit(solution)/shard_map/while/body/eval_jaxpr/qd,kd->qk/dot_general | solution.py:16
  686.9 18.3 %multiply_convert_fusion.9 = bf16[2304,2304]{0,1:T(8,128)(2,1)} fusion(f32[2304,2304]{0,1:T(8,128)} %get-tuple-element.318, f32[2304,2304]{0,1:T(8,128)} %fusion.152, f32[2304]{0:T(1024)S(1)} %get-tuple-element.319), kind=kLoop, calls=%fused_computation.19.clone.1 | loop fusion | flops 15925248 | bytes 53093376 | tf_op jit(solution)/shard_map/while/body/eval_jaxpr/convert_element_type | solution.py:55
  744.0 22.1 %psum.60 = f32[384]{0:T(512)S(1)} all-reduce(f32[384]{0:T(512)} %get-tuple-element.228), channel_id=1, replica_groups=mesh['dp'=8,'tp'=4] {'dp'}, use_global_device_ids=true, to_apply=%region_22.23 | all-reduce | flops 384 | bytes 3072 | tf_op jit(solution)/shard_map/psum | solution.py:202
  770.4 58.2 %all-reduce.7.cloned.1.call-done = (f32[3,384,96]{1,2,0:T(8,128)}, f32[96,384]{1,0:T(8,128)}, f32[384,384]{1,0:T(8,128)}, f32[384,384]{1,0:T(8,128)}) async-done(((f32[3,384,96]{1,2,0:T(8,128)}, f32[96,384]{1,0:T(8,128)}, f32[384,384]{1,0:T(8,128)}, f32[384,384]{1,0:T(8,128)}), (f32[3,384,96]{1,2,0:T(8,128)}, f32[96,384]{1,0:T(8,128)}, f32[384,384]{1,0:T(8,128)}, ...) | async-done | bytes 1769488 | tf_op jit(solution)/shard_map/psum | solution.py:202
  836.3 35.0 %reduce-scatter.11.cloned.1.call-done = bf16[2,576,384]{2,1,0:T(8,128)(2,1)} async-done(((bf16[2,2304,384]{2,1,0:T(8,128)(2,1)}), bf16[2,576,384]{2,1,0:T(8,128)(2,1)}) %reduce-scatter.11.cloned.1.call-update) | async-done | bytes 884752 | tf_op jit(solution)/shard_map/reduce_scatter | solution.py:179
  874.8 39.9 %all-reduce = (f32[]{:T(128)}, f32[9,384]{1,0:T(8,128)}) all-reduce(f32[]{:T(128)S(6)} %div.48, f32[9,384]{1,0:T(8,128)S(1)} %stack.61), channel_id=1, replica_groups=mesh['dp'=8,'tp'=4] {'dp','tp'}, use_global_device_ids=true, to_apply=%region_11.12 | all-reduce | flops 3457 | bytes 27656 | tf_op jit(solution)/shard_map/psum | solution.py:205
  (305 shorter events, 290.8 us)
Async XLA Ops:
  7.2 229.1 %copy-start = (bf16[2,576,384]{2,1,0:T(8,128)(2,1)S(1)}, bf16[2,576,384]{2,1,0:T(8,128)(2,1)}, u32[]{:S(2)}) copy-start(bf16[2,576,384]{2,1,0:T(8,128)(2,1)} %param.30) | copy-start | bytes 2654212
  7.2 40.6 %all-gather.5.cloned.1.call-start = ((), (), s32[]{:S(2)}) async-start(), calls=%async_computation.4 | async-start | bytes 4423680 | tf_op jit(solution)/shard_map/all_gather | solution.py:121
  14.2 174.4 %reduce-scatter.5.cloned.1.call-start = ((), (), s32[]{:S(2)}) async-start(), calls=%async_computation.5 | async-start | bytes 8847360 | tf_op jit(solution)/shard_map/reduce_scatter | solution.py:126
  124.8 63.8 %copy-start.57 = (f32[384]{0:T(512)S(1)}, f32[384]{0:T(512)}, u32[]{:S(2)}) copy-start(f32[384]{0:T(512)} %get-tuple-element.152) | copy-start | bytes 4612
  124.9 98.4 %all-gather.7.cloned.1.call-start = ((), (), s32[]{:S(2)}) async-start(), calls=%async_computation.6 | async-start | bytes 4423680 | tf_op jit(solution)/shard_map/all_gather | solution.py:134
  192.4 107.0 %reduce-scatter.7.cloned.1.call-start = ((), (), s32[]{:S(2)}) async-start(), calls=%async_computation.7 | async-start | bytes 8847360 | tf_op jit(solution)/shard_map/reduce_scatter | solution.py:137
  235.4 63.9 %copy-start.55 = (f32[384]{0:T(512)S(1)}, f32[384]{0:T(512)}, u32[]{:S(2)}) copy-start(f32[384]{0:T(512)} %get-tuple-element.148) | copy-start | bytes 4612
  235.4 63.9 %copy-start.56 = (f32[384]{0:T(512)S(1)}, f32[384]{0:T(512)}, u32[]{:S(2)}) copy-start(f32[384]{0:T(512)} %get-tuple-element.151) | copy-start | bytes 4612
  235.4 102.3 %all-gather.9.cloned.1.call-start = ((), (), s32[]{:S(2)}) async-start(), calls=%async_computation.8 | async-start | bytes 4423680 | tf_op jit(solution)/shard_map/all_gather | solution.py:155
  306.8 110.9 %reduce-scatter.9.cloned.1.call-start = ((), (), s32[]{:S(2)}) async-start(), calls=%async_computation.9 | async-start | bytes 8847360 | tf_op jit(solution)/shard_map/reduce_scatter | solution.py:161
  353.8 103.2 %all-gather.11.cloned.1.call-start = ((), (), s32[]{:S(2)}) async-start(), calls=%async_computation.10 | async-start | bytes 4423680 | tf_op jit(solution)/shard_map/all_gather | solution.py:172
  426.1 315.3 %all-reduce.5.cloned.1.call-start = ((), (), s32[]{:S(2)}) async-start(), calls=%async_computation.11 | async-start | bytes 1179648 | tf_op jit(solution)/shard_map/psum | solution.py:205
  427.7 400.9 %all-reduce.7.cloned.1.call-start = ((), (), s32[]{:S(2)}) async-start(), calls=%async_computation.13 | async-start | bytes 3538944 | tf_op jit(solution)/shard_map/psum | solution.py:202
  733.5 137.8 %reduce-scatter.11.cloned.1.call-start = ((), (), s32[]{:S(2)}) async-start(), calls=%async_computation.12 | async-start | bytes 4423680 | tf_op jit(solution)/shard_map/reduce_scatter | solution.py:179
  738.5 90.1 %copy-start.25 = (f32[96,384]{1,0:T(8,128)S(1)}, f32[96,384]{1,0:T(8,128)}, u32[]{:S(2)}) copy-start(f32[96,384]{1,0:T(8,128)} %param.34) | copy-start | bytes 442372
  738.5 90.1 %copy-start.45 = (f32[96,384]{1,0:T(8,128)S(1)}, f32[96,384]{1,0:T(8,128)}, u32[]{:S(2)}) copy-start(f32[96,384]{1,0:T(8,128)} %param.48) | copy-start | bytes 442372
  738.5 90.1 %copy-start.46 = (f32[96,384]{1,0:T(8,128)S(1)}, f32[96,384]{1,0:T(8,128)}, u32[]{:S(2)}) copy-start(f32[96,384]{1,0:T(8,128)} %param.41) | copy-start | bytes 442372
  741.4 89.0 %copy-start.42 = (f32[3,384,96]{1,2,0:T(8,128)S(1)}, f32[3,384,96]{1,2,0:T(8,128)}, u32[]{:S(2)}) copy-start(f32[3,384,96]{1,2,0:T(8,128)} %param.33) | copy-start | bytes 1327108
  741.4 89.0 %copy-start.43 = (f32[3,384,96]{1,2,0:T(8,128)S(1)}, f32[3,384,96]{1,2,0:T(8,128)}, u32[]{:S(2)}) copy-start(f32[3,384,96]{1,2,0:T(8,128)} %param.47) | copy-start | bytes 1327108
  741.4 89.0 %copy-start.44 = (f32[3,384,96]{1,2,0:T(8,128)S(1)}, f32[3,384,96]{1,2,0:T(8,128)}, u32[]{:S(2)}) copy-start(f32[3,384,96]{1,2,0:T(8,128)} %param.40) | copy-start | bytes 1327108
  744.0 88.6 %copy-start.20 = (f32[384,384]{1,0:T(8,128)S(1)}, f32[384,384]{1,0:T(8,128)}, u32[]{:S(2)}) copy-start(f32[384,384]{1,0:T(8,128)} %param.35) | copy-start | bytes 1769476
  744.0 88.6 %copy-start.33 = (f32[384,384]{1,0:T(8,128)S(1)}, f32[384,384]{1,0:T(8,128)}, u32[]{:S(2)}) copy-start(f32[384,384]{1,0:T(8,128)} %param.49) | copy-start | bytes 1769476
  744.0 88.6 %copy-start.34 = (f32[384,384]{1,0:T(8,128)S(1)}, f32[384,384]{1,0:T(8,128)}, u32[]{:S(2)}) copy-start(f32[384,384]{1,0:T(8,128)} %param.42) | copy-start | bytes 1769476
  834.9 81.3 %copy-start.13 = (f32[2,576,384]{2,1,0:T(8,128)S(1)}, f32[2,576,384]{2,1,0:T(8,128)}, u32[]{:S(2)}) copy-start(f32[2,576,384]{2,1,0:T(8,128)} %copy-done.12) | copy-start | bytes 5308420
  (69 other events, 1141.6 us)
Sparse Core Ops, SparseCore 0:
  14.4 33.4 all-gather.4
  125.0 63.6 reduce-scatter.4
  192.5 30.7 all-gather.6
  235.6 63.7 reduce-scatter.6
  306.9 30.7 all-gather.8
  353.9 63.6 reduce-scatter.8
  426.3 30.7 all-gather.10
  463.7 127.3 all-reduce.4
  733.6 95.0 all-reduce.6
  831.2 40.0 reduce-scatter.10
where the time goes:
time: 936 us; the launch traced here: 926 us
  waiting for transfers between devices  396 us (42%)
  matrix products  282 us (30%)
  other arithmetic  126 us (13%)
  blocking collectives  62 us (7%)
  local copies, waits for them, and re-layouts  44 us (5%)
  between operations  15.7 us (2%)
    dot_general x43, matrix products, product(): return jnp.einsum(form, left, right, preferred_element_type=jnp.float32)  282 us
    convert_element_type x4, other arithmetic, head_backward(): grad_scores = (probs * (grad_probs - jnp.sum(probs * grad_probs, axis=-1,...  73.3 us
    reduce_scatter x1, waiting for transfers between devices, per_device(): lax.psum_scatter(product(grad_pre, up_all, 'bsf,df->bsd'), 'tp', scatter_...  63.8 us
    reduce_scatter x1, waiting for transfers between devices, per_device(): lax.psum_scatter(product(attended, out_low, 'bse,ed->bsd'), 'tp', scatter...  63.7 us
    reduce_scatter x1, waiting for transfers between devices, per_device(): lax.psum_scatter(product(hidden, down_all, 'bsf,df->bsd'), 'tp', scatter_...  61.4 us
    psum x1, waiting for transfers between devices, per_device(): lax.psum((grad_attn_proj, grad_out, grad_up, grad_up_bias, grad_down), 'dp')  58.2 us
    psum x1, blocking collectives, per_device(): lax.psum((grad_head, grad_vectors, part_loss), ('dp', 'tp'))  39.9 us
    reduce_scatter x1, waiting for transfers between devices, per_device(): lax.psum_scatter(product(grad_packed, attn_low, 'jbse,jde->bsd').astype(j...  35 us
  transfers between devices with their start and end apart: 10, of which 9 were waited for; matrix products, arithmetic and copies ran while one was open for 33% of the time, Pallas kernels for 0%

commit v1 on v0

--- a/solution.py
+++ b/solution.py
@@ -2,6 +2,7 @@
 import jax.numpy as jnp
 from jax import lax
 from jax.sharding import PartitionSpec as P
+from jax.lax import axis_index, axis_size, ppermute
 
 CHN = 96
 HDIM = 48
@@ -131,7 +132,29 @@
     second_low = second.astype(bf16)
     up_all = up_proj.astype(bf16)
     down_all = down_proj.astype(bf16)
-    second_all = lax.all_gather(second_low, "tp", axis=1, tiled=True)
+    wide_out, kept_arr, then = (axis_size("tp"), axis_index("tp"), second_low.shape[1])
+    xs_all = []
+    for dev in range(wide_out):
+        xs_all.append((dev, (dev + 1) % wide_out))
+    sides = []
+    for dev in range(wide_out):
+        sides.append((dev, (dev - 1) % wide_out))
+    second_all = jnp.zeros(
+        (*second_low.shape[:1], wide_out * then, *second_low.shape[2:]), second_low.dtype
+    )
+    second_all = lax.dynamic_update_slice_in_dim(second_all, second_low, kept_arr * then, axis=1)
+    block_next = main = second_low
+    t_next = wide_out // 2
+    for k0 in range(1, t_next + 1):
+        block_next = ppermute(block_next, "tp", xs_all)
+        second_all = lax.dynamic_update_slice_in_dim(
+            second_all, block_next, (kept_arr - k0) % wide_out * then, axis=1
+        )
+        if k0 < wide_out - t_next:
+            main = ppermute(main, "tp", sides)
+            second_all = lax.dynamic_update_slice_in_dim(
+                second_all, main, (kept_arr + k0) % wide_out * then, axis=1
+            )
     hidden_pre = product(second_all, up_all, "bsd,df->bsf") + up_bias
     hidden = jax.nn.gelu(hidden_pre).astype(bf16)
     ffn_term = lax.psum_scatter(

time: 936 us -> 983 us (1.050)
  local copies, waits for them, and re-layouts: 44 us -> 98.4 us
  waiting for transfers between devices: 396 us -> 382 us
    dynamic_update_slice x0 -> x4, local copies, waits for them, and re-layouts: none -> 43.4 us  [the longest x2 21.3 us: per_device(): lax.dynamic_update_slice_in_dim(second_all, block_next, (kept_arr - k0) %...]
    all_gather x1 -> x0, waiting for transfers between devices: 30.7 us -> none  [per_device(): second_all = lax.all_gather(second_low, 'tp', axis=1, tiled=True)]
    ppermute x0 -> x3, waiting for transfers between devices: none -> 19.7 us  [the longest x2 19.7 us: per_device(): block_next = ppermute(block_next, 'tp', xs_all)]
  transfers between devices with their start and end apart: 10 -> 12, of which waited for: 9 -> 9; matrix products, arithmetic and copies ran while one was open for 33% -> 36% of each run, Pallas kernels for 0% -> 0%
where the time goes in v1:
time: 983 us; the launch traced here: 971 us
  waiting for transfers between devices  382 us (39%)
  matrix products  284 us (29%)
  other arithmetic  126 us (13%)
  local copies, waits for them, and re-layouts  98.4 us (10%)
  blocking collectives  61.9 us (6%)
  between operations  15.5 us (2%)
    dot_general x43, matrix products, product(): return jnp.einsum(form, left, right, preferred_element_type=jnp.float32)  284 us
    convert_element_type x4, other arithmetic, head_backward(): grad_scores = (probs * (grad_probs - jnp.sum(probs * grad_probs, axis=-1,...  73.3 us
    reduce_scatter x1, waiting for transfers between devices, per_device(): lax.psum_scatter(product(attended, out_low, 'bse,ed->bsd'), 'tp', scatter...  63.8 us
    reduce_scatter x1, waiting for transfers between devices, per_device(): lax.psum_scatter(product(grad_pre, up_all, 'bsf,df->bsd'), 'tp', scatter_...  63.8 us
    reduce_scatter x1, waiting for transfers between devices, per_device(): lax.psum_scatter(product(hidden, down_all, 'bsf,df->bsd'), 'tp', scatter_...  62.2 us
    psum x1, waiting for transfers between devices, per_device(): lax.psum((grad_attn_proj, grad_out, grad_up, grad_up_bias, grad_down), 'dp')  57.3 us
    psum x1, blocking collectives, per_device(): lax.psum((grad_head, grad_vectors, part_loss), ('dp', 'tp'))  39.9 us
    reduce_scatter x1, waiting for transfers between devices, per_device(): lax.psum_scatter(product(grad_packed, attn_low, 'jbse,jde->bsd').astype(j...  35.2 us
  transfers between devices with their start and end apart: 12, of which 9 were waited for; matrix products, arithmetic and copies ran while one was open for 36% of the time, Pallas kernels for 0%

profile of v1, /device:TPU:0, one launch (start us, length us, event | category | flops | bytes accessed | tf_op | source)
XLA Modules:
  0.0 971.3 jit_solution(814647472654936825)
XLA Ops:
  15.5 33.5 %all-gather.4.cloned.1.call-done = bf16[2,2304,384]{2,1,0:T(8,128)(2,1)} async-done(((bf16[2,576,384]{2,1,0:T(8,128)(2,1)}), bf16[2,2304,384]{2,1,0:T(8,128)(2,1)}) %all-gather.4.cloned.1.call-update) | async-done | bytes 3538960 | tf_op jit(solution)/shard_map/all_gather | solution.py:122
  62.9 57.2 %while.22 = (s32[]{:T(128)}, bf16[4,2304,48]{1,2,0:T(8,128)(2,1)}, f32[4,2304]{1,0:T(4,128)}, bf16[4,2304,48]{2,1,0:T(8,128)(2,1)S(1)}, bf16[4,2304,48]{2,1,0:T(...) while((s32[]{:T(128)}, bf16[4,2304,48]{1,2,0:T(8,128)(2,1)}, f32[4,2304]{1,0:T(4,128)}, ...), condition=%wide.region_5.6_spmd, body=%wide.region_2.0_spmd.sunk | while | flops 1056483072 | bytes 65804384 | solution.py:125
  126.1 63.8 %reduce-scatter.5.cloned.1.call-done = f32[2,576,384]{2,1,0:T(8,128)} async-done(((f32[2,2304,384]{2,1,0:T(8,128)}), f32[2,576,384]{2,1,0:T(8,128)}) %reduce-scatter.5.cloned.1.call-update) | async-done | bytes 1769488 | tf_op jit(solution)/shard_map/reduce_scatter | solution.py:127
  194.5 19.7 %collective-permute-done = bf16[2,576,384]{2,1,0:T(8,128)(2,1)} collective-permute-done((bf16[2,576,384]{2,1,0:T(8,128)(2,1)S(1)}, bf16[2,576,384]{2,1,0:T(8,128)(2,1)}, u32[]{:S(2)}, u32[]{:S(2)}) %collective-permute-start) | collective-permute-done | bytes 884768 | tf_op jit(solution)/shard_map/ppermute | solution.py:149
  243.6 11.6 %dynamic_update_slice.26 = bf16[2,2304,384]{1,2,0:T(8,128)(2,1)} dynamic-update-slice(bf16[2,2304,384]{1,2,0:T(8,128)(2,1)} %dynamic_update_slice.25, bf16[2,576,384]{1,2,0:T(8,128)(2,1)} %copy.98, s32[]{:T(128)} %copy.146, s32[]{:T(128)S(6)} %select_n.51, s32[]{:T(128)} %copy.146) | dynamic-update-slice | bytes 1769476 | tf_op jit(solution)/shard_map/dynamic_update_slice | solution.py:155
  282.5 62.2 %reduce-scatter.7.cloned.1.call-done = f32[2,576,384]{2,1,0:T(8,128)} async-done(((f32[2,2304,384]{2,1,0:T(8,128)}), f32[2,576,384]{2,1,0:T(8,128)}) %reduce-scatter.7.cloned.1.call-update) | async-done | bytes 1769488 | tf_op jit(solution)/shard_map/reduce_scatter | solution.py:160
  352.5 30.7 %all-gather.6.cloned.1.call-done = bf16[2,2304,384]{2,1,0:T(8,128)(2,1)} async-done(((bf16[2,576,384]{2,1,0:T(8,128)(2,1)}), bf16[2,2304,384]{2,1,0:T(8,128)(2,1)}) %all-gather.6.cloned.1.call-update) | async-done | bytes 3538960 | tf_op jit(solution)/shard_map/all_gather | solution.py:178
  399.3 63.8 %reduce-scatter.9.cloned.1.call-done = f32[2,576,384]{2,1,0:T(8,128)} async-done(((f32[2,2304,384]{2,1,0:T(8,128)}), f32[2,576,384]{2,1,0:T(8,128)}) %reduce-scatter.9.cloned.1.call-update) | async-done | bytes 1769488 | tf_op jit(solution)/shard_map/reduce_scatter | solution.py:184
  486.8 15.7 %all-gather.8.cloned.1.call-done = bf16[2,2304,384]{2,1,0:T(8,128)(2,1)} async-done(((bf16[2,576,384]{2,1,0:T(8,128)(2,1)}), bf16[2,2304,384]{2,1,0:T(8,128)(2,1)}) %all-gather.8.cloned.1.call-update) | async-done | bytes 3538960 | tf_op jit(solution)/shard_map/all_gather | solution.py:195
  508.9 263.6 %while.23 = (s32[]{:T(128)}, bf16[4,3,2304,48]{2,3,1,0:T(8,128)(2,1)}, bf16[4,2304,48]{2,1,0:T(8,128)(2,1)S(1)}, bf16[4,2304,48]{2,1,0:T(8,128)(2,1)}, f32[4,230...) while((s32[]{:T(128)}, ...), condition=%wide.region_17.18_spmd, body=%wide.region_15.17_spmd.sunk | while | flops 2593048320 | bytes 211429520 | solution.py:199
  509.7 11.4 %fusion.152 = f32[2304,2304]{0,1:T(8,128)} fusion(bf16[4,2304,48]{2,1,0:T(8,128)(2,1)} %get-tuple-element.366, s32[]{:T(128)S(6)} %copy.136, bf16[4,2304,48]{2,1,0:T(8,128)(2,1)} %get-tuple-element.365), kind=kOutput, calls=%fused_computation.33.clone.1 | convolution fusion | flops 509607936 | bytes 22414336 | tf_op jit(solution)/shard_map/while/body/eval_jaxpr/qd,kd->qk/dot_general | solution.py:17
  521.1 13.7 %multiply_reduce_fusion.11 = (f32[2304]{0:T(1024)S(1)}, f32[2304,2304]{0,1:T(8,128)}) fusion(f32[2304,2304]{0,1:T(8,128)} %fusion.152, f32[2304]{0:T(1024)S(1)} %dynamic-slice_reduce_fusion.2, bf16[4,2304,48]{2,1,0:T(8,128)(2,1)S(1)} %copy-done.5, s32[]{:T(128)S(6)} %copy.136, bf16[4,2304,48]{2,1,0:T(8,128)(2,1)S(1)} %get-tuple-element.362), kind=kOutput, calls=%fused_computation.20.clone.1 | convolution fusion | flops 530839296 | bytes 43669504 | tf_op jit(solution)/shard_map/while/body/eval_jaxpr/qd,kd->qk/dot_general | solution.py:17
  534.8 18.4 %multiply_convert_fusion.9 = bf16[2304,2304]{0,1:T(8,128)(2,1)} fusion(f32[2304,2304]{0,1:T(8,128)} %get-tuple-element.318, f32[2304,2304]{0,1:T(8,128)} %fusion.152, f32[2304]{0:T(1024)S(1)} %get-tuple-element.319), kind=kLoop, calls=%fused_computation.19.clone.1 | loop fusion | flops 15925248 | bytes 53093376 | tf_op jit(solution)/shard_map/while/body/eval_jaxpr/convert_element_type | solution.py:56
  575.8 11.4 %fusion.152 = f32[2304,2304]{0,1:T(8,128)} fusion(bf16[4,2304,48]{2,1,0:T(8,128)(2,1)} %get-tuple-element.366, s32[]{:T(128)S(6)} %copy.136, bf16[4,2304,48]{2,1,0:T(8,128)(2,1)} %get-tuple-element.365), kind=kOutput, calls=%fused_computation.33.clone.1 | convolution fusion | flops 509607936 | bytes 22414336 | tf_op jit(solution)/shard_map/while/body/eval_jaxpr/qd,kd->qk/dot_general | solution.py:17
  587.2 13.6 %multiply_reduce_fusion.11 = (f32[2304]{0:T(1024)S(1)}, f32[2304,2304]{0,1:T(8,128)}) fusion(f32[2304,2304]{0,1:T(8,128)} %fusion.152, f32[2304]{0:T(1024)S(1)} %dynamic-slice_reduce_fusion.2, bf16[4,2304,48]{2,1,0:T(8,128)(2,1)S(1)} %copy-done.5, s32[]{:T(128)S(6)} %copy.136, bf16[4,2304,48]{2,1,0:T(8,128)(2,1)S(1)} %get-tuple-element.362), kind=kOutput, calls=%fused_computation.20.clone.1 | convolution fusion | flops 530839296 | bytes 43669504 | tf_op jit(solution)/shard_map/while/body/eval_jaxpr/qd,kd->qk/dot_general | solution.py:17
  600.8 18.4 %multiply_convert_fusion.9 = bf16[2304,2304]{0,1:T(8,128)(2,1)} fusion(f32[2304,2304]{0,1:T(8,128)} %get-tuple-element.318, f32[2304,2304]{0,1:T(8,128)} %fusion.152, f32[2304]{0:T(1024)S(1)} %get-tuple-element.319), kind=kLoop, calls=%fused_computation.19.clone.1 | loop fusion | flops 15925248 | bytes 53093376 | tf_op jit(solution)/shard_map/while/body/eval_jaxpr/convert_element_type | solution.py:56
  653.2 13.5 %multiply_reduce_fusion.11 = (f32[2304]{0:T(1024)S(1)}, f32[2304,2304]{0,1:T(8,128)}) fusion(f32[2304,2304]{0,1:T(8,128)} %fusion.152, f32[2304]{0:T(1024)S(1)} %dynamic-slice_reduce_fusion.2, bf16[4,2304,48]{2,1,0:T(8,128)(2,1)S(1)} %copy-done.5, s32[]{:T(128)S(6)} %copy.136, bf16[4,2304,48]{2,1,0:T(8,128)(2,1)S(1)} %get-tuple-element.362), kind=kOutput, calls=%fused_computation.20.clone.1 | convolution fusion | flops 530839296 | bytes 43669504 | tf_op jit(solution)/shard_map/while/body/eval_jaxpr/qd,kd->qk/dot_general | solution.py:17
  666.7 18.3 %multiply_convert_fusion.9 = bf16[2304,2304]{0,1:T(8,128)(2,1)} fusion(f32[2304,2304]{0,1:T(8,128)} %get-tuple-element.318, f32[2304,2304]{0,1:T(8,128)} %fusion.152, f32[2304]{0:T(1024)S(1)} %get-tuple-element.319), kind=kLoop, calls=%fused_computation.19.clone.1 | loop fusion | flops 15925248 | bytes 53093376 | tf_op jit(solution)/shard_map/while/body/eval_jaxpr/convert_element_type | solution.py:56
  718.9 13.5 %multiply_reduce_fusion.11 = (f32[2304]{0:T(1024)S(1)}, f32[2304,2304]{0,1:T(8,128)}) fusion(f32[2304,2304]{0,1:T(8,128)} %fusion.152, f32[2304]{0:T(1024)S(1)} %dynamic-slice_reduce_fusion.2, bf16[4,2304,48]{2,1,0:T(8,128)(2,1)S(1)} %copy-done.5, s32[]{:T(128)S(6)} %copy.136, bf16[4,2304,48]{2,1,0:T(8,128)(2,1)S(1)} %get-tuple-element.362), kind=kOutput, calls=%fused_computation.20.clone.1 | convolution fusion | flops 530839296 | bytes 43669504 | tf_op jit(solution)/shard_map/while/body/eval_jaxpr/qd,kd->qk/dot_general | solution.py:17
  732.4 18.3 %multiply_convert_fusion.9 = bf16[2304,2304]{0,1:T(8,128)(2,1)} fusion(f32[2304,2304]{0,1:T(8,128)} %get-tuple-element.318, f32[2304,2304]{0,1:T(8,128)} %fusion.152, f32[2304]{0:T(1024)S(1)} %get-tuple-element.319), kind=kLoop, calls=%fused_computation.19.clone.1 | loop fusion | flops 15925248 | bytes 53093376 | tf_op jit(solution)/shard_map/while/body/eval_jaxpr/convert_element_type | solution.py:56
  789.8 21.9 %psum.60 = f32[384]{0:T(512)S(1)} all-reduce(f32[384]{0:T(512)} %get-tuple-element.228), channel_id=1, replica_groups=mesh['dp'=8,'tp'=4] {'dp'}, use_global_device_ids=true, to_apply=%region_22.23 | all-reduce | flops 384 | bytes 3072 | tf_op jit(solution)/shard_map/psum | solution.py:225
  816.7 57.3 %all-reduce.7.cloned.1.call-done = (f32[3,384,96]{1,2,0:T(8,128)}, f32[96,384]{1,0:T(8,128)}, f32[384,384]{1,0:T(8,128)}, f32[384,384]{1,0:T(8,128)}) async-done(((f32[3,384,96]{1,2,0:T(8,128)}, f32[96,384]{1,0:T(8,128)}, f32[384,384]{1,0:T(8,128)}, f32[384,384]{1,0:T(8,128)}), (f32[3,384,96]{1,2,0:T(8,128)}, f32[96,384]{1,0:T(8,128)}, f32[384,384]{1,0:T(8,128)}, ...) | async-done | bytes 1769488 | tf_op jit(solution)/shard_map/psum | solution.py:225
  881.6 35.2 %reduce-scatter.11.cloned.1.call-done = bf16[2,576,384]{2,1,0:T(8,128)(2,1)} async-done(((bf16[2,2304,384]{2,1,0:T(8,128)(2,1)}), bf16[2,576,384]{2,1,0:T(8,128)(2,1)}) %reduce-scatter.11.cloned.1.call-update) | async-done | bytes 884752 | tf_op jit(solution)/shard_map/reduce_scatter | solution.py:202
  920.4 39.9 %all-reduce = (f32[]{:T(128)}, f32[9,384]{1,0:T(8,128)}) all-reduce(f32[]{:T(128)S(6)} %div.48, f32[9,384]{1,0:T(8,128)S(1)} %stack.61), channel_id=1, replica_groups=mesh['dp'=8,'tp'=4] {'dp','tp'}, use_global_device_ids=true, to_apply=%region_11.12 | all-reduce | flops 3457 | bytes 27656 | tf_op jit(solution)/shard_map/psum | solution.py:228
  (315 shorter events, 349.5 us)
Async XLA Ops:
  7.2 273.7 %copy-start = (bf16[2,576,384]{2,1,0:T(8,128)(2,1)S(1)}, bf16[2,576,384]{2,1,0:T(8,128)(2,1)}, u32[]{:S(2)}) copy-start(bf16[2,576,384]{2,1,0:T(8,128)(2,1)} %param.30) | copy-start | bytes 2654212
  7.2 41.8 %all-gather.4.cloned.1.call-start = ((), (), s32[]{:S(2)}) async-start(), calls=%async_computation.4 | async-start | bytes 4423680 | tf_op jit(solution)/shard_map/all_gather | solution.py:122
  15.4 174.5 %reduce-scatter.5.cloned.1.call-start = ((), (), s32[]{:S(2)}) async-start(), calls=%async_computation.5 | async-start | bytes 8847360 | tf_op jit(solution)/shard_map/reduce_scatter | solution.py:127
  126.0 218.7 %reduce-scatter.7.cloned.1.call-start = ((), (), s32[]{:S(2)}) async-start(), calls=%async_computation.6 | async-start | bytes 8847360 | tf_op jit(solution)/shard_map/reduce_scatter | solution.py:160
  192.7 21.5 %collective-permute-start = (bf16[2,576,384]{2,1,0:T(8,128)(2,1)S(1)}, bf16[2,576,384]{2,1,0:T(8,128)(2,1)}, u32[]{:S(2)}, u32[]{:S(2)}) collective-permute-start(bf16[2,576,384]{2,1,0:T(8,128)(2,1)S(1)} %add_convert_fusion.1), channel_id=1, source_target_pairs={{0,1},{1,2},{2,3},{3,0},{4,5},{5,6},{6,7},{7,4},{8,9},{9,10},{10,1... | collective-permute-start | bytes 2654216 | tf_op jit(solution)/shard_map/ppermute | solution.py:149
  192.8 48.6 %collective-permute-start.1 = (bf16[2,576,384]{2,1,0:T(8,128)(2,1)S(1)}, bf16[2,576,384]{2,1,0:T(8,128)(2,1)}, u32[]{:S(2)}, u32[]{:S(2)}) collective-permute-start(bf16[2,576,384]{2,1,0:T(8,128)(2,1)S(1)} %add_convert_fusion.1), channel_id=1, source_target_pairs={{0,3},{1,0},{2,1},{3,2},{4,7},{5,4},{6,5},{7,6},{8,11},{9,8},{10,9... | collective-permute-start | bytes 2654216 | tf_op jit(solution)/shard_map/ppermute | solution.py:154
  214.2 41.0 %collective-permute-start.2 = (bf16[2,576,384]{2,1,0:T(8,128)(2,1)}, bf16[2,576,384]{2,1,0:T(8,128)(2,1)}, u32[]{:S(2)}, u32[]{:S(2)}) collective-permute-start(bf16[2,576,384]{2,1,0:T(8,128)(2,1)} %collective-permute-done), channel_id=1, source_target_pairs={{0,1},{1,2},{2,3},{3,0},{4,5},{5,6},{6,7},{7,4},{8,9},{9,10},{10,1... | collective-permute-start | bytes 2654216 | tf_op jit(solution)/shard_map/ppermute | solution.py:149
  280.1 103.1 %all-gather.6.cloned.1.call-start = ((), (), s32[]{:S(2)}) async-start(), calls=%async_computation.7 | async-start | bytes 4423680 | tf_op jit(solution)/shard_map/all_gather | solution.py:178
  352.2 110.9 %reduce-scatter.9.cloned.1.call-start = ((), (), s32[]{:S(2)}) async-start(), calls=%async_computation.8 | async-start | bytes 8847360 | tf_op jit(solution)/shard_map/reduce_scatter | solution.py:184
  399.2 66.9 %copy-start.51 = (f32[384]{0:T(512)S(1)}, f32[384]{0:T(512)}, u32[]{:S(2)}) copy-start(f32[384]{0:T(512)} %get-tuple-element.155) | copy-start | bytes 4612
  399.2 103.3 %all-gather.8.cloned.1.call-start = ((), (), s32[]{:S(2)}) async-start(), calls=%async_computation.9 | async-start | bytes 4423680 | tf_op jit(solution)/shard_map/all_gather | solution.py:195
  471.6 315.8 %all-reduce.5.cloned.1.call-start = ((), (), s32[]{:S(2)}) async-start(), calls=%async_computation.10 | async-start | bytes 1179648 | tf_op jit(solution)/shard_map/psum | solution.py:228
  473.2 400.9 %all-reduce.7.cloned.1.call-start = ((), (), s32[]{:S(2)}) async-start(), calls=%async_computation.12 | async-start | bytes 3538944 | tf_op jit(solution)/shard_map/psum | solution.py:225
  779.0 137.8 %reduce-scatter.11.cloned.1.call-start = ((), (), s32[]{:S(2)}) async-start(), calls=%async_computation.11 | async-start | bytes 4423680 | tf_op jit(solution)/shard_map/reduce_scatter | solution.py:202
  784.0 90.0 %copy-start.22 = (f32[96,384]{1,0:T(8,128)S(1)}, f32[96,384]{1,0:T(8,128)}, u32[]{:S(2)}) copy-start(f32[96,384]{1,0:T(8,128)} %param.34) | copy-start | bytes 442372
  784.0 90.0 %copy-start.42 = (f32[96,384]{1,0:T(8,128)S(1)}, f32[96,384]{1,0:T(8,128)}, u32[]{:S(2)}) copy-start(f32[96,384]{1,0:T(8,128)} %param.48) | copy-start | bytes 442372
  784.0 90.0 %copy-start.43 = (f32[96,384]{1,0:T(8,128)S(1)}, f32[96,384]{1,0:T(8,128)}, u32[]{:S(2)}) copy-start(f32[96,384]{1,0:T(8,128)} %param.41) | copy-start | bytes 442372
  784.0 91.8 %copy-start.39 = (f32[3,384,96]{1,2,0:T(8,128)S(1)}, f32[3,384,96]{1,2,0:T(8,128)}, u32[]{:S(2)}) copy-start(f32[3,384,96]{1,2,0:T(8,128)} %param.33) | copy-start | bytes 1327108
  784.0 91.8 %copy-start.40 = (f32[3,384,96]{1,2,0:T(8,128)S(1)}, f32[3,384,96]{1,2,0:T(8,128)}, u32[]{:S(2)}) copy-start(f32[3,384,96]{1,2,0:T(8,128)} %param.47) | copy-start | bytes 1327108
  784.1 91.8 %copy-start.41 = (f32[3,384,96]{1,2,0:T(8,128)S(1)}, f32[3,384,96]{1,2,0:T(8,128)}, u32[]{:S(2)}) copy-start(f32[3,384,96]{1,2,0:T(8,128)} %param.40) | copy-start | bytes 1327108
  789.8 88.2 %copy-start.16 = (f32[384,384]{1,0:T(8,128)S(1)}, f32[384,384]{1,0:T(8,128)}, u32[]{:S(2)}) copy-start(f32[384,384]{1,0:T(8,128)} %param.35) | copy-start | bytes 1769476
  789.8 88.2 %copy-start.30 = (f32[384,384]{1,0:T(8,128)S(1)}, f32[384,384]{1,0:T(8,128)}, u32[]{:S(2)}) copy-start(f32[384,384]{1,0:T(8,128)} %param.49) | copy-start | bytes 1769476
  789.8 88.2 %copy-start.31 = (f32[384,384]{1,0:T(8,128)S(1)}, f32[384,384]{1,0:T(8,128)}, u32[]{:S(2)}) copy-start(f32[384,384]{1,0:T(8,128)} %param.42) | copy-start | bytes 1769476
  880.3 81.5 %copy-start.9 = (f32[2,576,384]{2,1,0:T(8,128)S(1)}, f32[2,576,384]{2,1,0:T(8,128)}, u32[]{:S(2)}) copy-start(f32[2,576,384]{2,1,0:T(8,128)} %copy-done.8) | copy-start | bytes 5308420
  (70 other events, 1387.6 us)
Sparse Core Ops, SparseCore 0:
  15.5 33.4 all-gather.3
  126.2 63.7 reduce-scatter.4
  280.2 64.4 reduce-scatter.6
  352.3 30.7 all-gather.5
  399.3 63.6 reduce-scatter.8
  471.7 30.8 all-gather.7
  509.2 127.2 all-reduce.4
  779.1 94.8 all-reduce.6
  876.8 40.0 reduce-scatter.10
